TPU v7x, 32 devices: a whole 2x2x4 slice. The times are simulated.
32 devices in a mesh: tm: 8 (over z, core), space: 4 (over y, x).
Axes of the slice: x: 2, y: 2, z: 4, core: 2. Of those that a mesh axis runs over, the one named last changes fastest.
Arguments:
- snapshots: bfloat16 [4096, 12288], P('tm', 'space')
- freq_ids: int32 [64], replicated, may hold values from 0 to 127
Outputs:
- gram: float32 [64, 2, 15, 15], P('tm')
All inputs are finite; a program needn't handle non-finite values.
Results may differ from a plain program's by a relative error of at most 0.00039.
Values may be sent and summed in bfloat16 or wider, within the bound.
No kernel may reach another device: no remote copies, remote signals or barrier semaphores. Data moves between devices by JAX's collectives and lax.ppermute only.
A program may use at most 64 MiB of HBM per device.

v0:
```python
import math
import jax
import jax.numpy as jnp
from jax import lax
from jax.sharding import PartitionSpec as P

NFFT = 512
F = 64


def shifted(block, axis, distance):
    devices = range(lax.axis_size(axis))
    route = [(i - distance, i) for i in devices if i - distance in devices]
    return lax.ppermute(block, axis, route)


def kernel_values(freqs, shifts, window_length):
    phase = freqs * shifts % window_length
    angle = 2.0 * math.pi / window_length * phase.astype(jnp.float32)
    window = 0.5 - 0.5 * jnp.cos(2.0 * math.pi / window_length * shifts.astype(jnp.float32))
    return (window * jnp.cos(angle), -window * jnp.sin(angle))


def local(snapshots, freq_ids):
    hop_len = NFFT // 2
    count_tm = lax.axis_size("tm")
    blocks = 2 * count_tm - 1
    device = lax.axis_index("tm")
    points = snapshots.shape[1]
    shifts = jnp.arange(NFFT, dtype=jnp.int32)
    real_part, imag_part = kernel_values(freq_ids[:, None], shifts[None, :], NFFT)
    table = jnp.stack([real_part, imag_part], axis=1).reshape(2 * F, NFFT).astype(jnp.bfloat16)
    leading = shifted(snapshots[:hop_len], "tm", -1)
    extended = jnp.concatenate([snapshots, leading], axis=0)
    pieces = []
    for slot in range(2):
        block = device * 2 + slot
        segment = extended[hop_len * slot : hop_len * slot + NFFT]
        result = jnp.dot(table, segment, preferred_element_type=jnp.float32)
        pieces.append(jnp.where(block < blocks, result, 0.0))
    owned = jnp.stack(pieces, axis=0).astype(jnp.bfloat16)
    owned = owned.reshape(2, F, 2, points)
    by_freq = lax.all_to_all(owned, "tm", split_axis=1, concat_axis=0, tiled=True)
    slots_all = by_freq.shape[0]
    resident_frequencies = by_freq.shape[1]
    stacked_snapshot_rows = jnp.transpose(by_freq, (1, 2, 0, 3)).reshape(
        resident_frequencies, 2 * slots_all, points
    )
    cross_product_terms = jnp.einsum(
        "tnf,tof->tno",
        stacked_snapshot_rows,
        stacked_snapshot_rows,
        preferred_element_type=jnp.float32,
    )
    gram_real_matrix = (
        cross_product_terms[:, :slots_all, :slots_all]
        + cross_product_terms[:, slots_all:, slots_all:]
    )
    imag_gram = (
        cross_product_terms[:, slots_all:, :slots_all]
        - cross_product_terms[:, :slots_all, slots_all:]
    )
    scale = 1.0 / (NFFT * points * lax.axis_size("space"))
    resident_gram_matrix = (
        jnp.stack([gram_real_matrix, imag_gram], axis=1)[:, :, :blocks, :blocks] * scale
    )
    return lax.psum(resident_gram_matrix, "space")


def solution(mesh):
    return jax.shard_map(
        local,
        mesh=mesh,
        in_specs=(P("tm", "space"), P()),
        out_specs=P("tm", None, None, None),
        check_vma=False,
    )
```

profile of v0, /device:TPU:0, one launch (start us, length us, event | category | flops | bytes accessed | tf_op | source)
XLA Modules:
  0.0 96.8 jit_solution(8468911311742353693)
XLA Ops:
  0.0 0.0 copy-start
  0.0 0.0 copy-start.2
  0.0 2.8 %slice.21 = bf16[256,3072]{1,0:T(8,128)(2,1)} slice(bf16[512,3072]{1,0:T(8,128)(2,1)} %param.2), slice={[0:256], [0:3072]} | slice | bytes 3145728 | tf_op jit(solution)/shard_map/slice | solution.py:33
  2.8 1.3 %collective-permute-start = (bf16[256,3072]{1,0:T(8,128)(2,1)}, bf16[256,3072]{1,0:T(8,128)(2,1)}, u32[]{:S(2)}, u32[]{:S(2)}) collective-permute-start(bf16[256,3072]{1,0:T(8,128)(2,1)} %slice.21), channel_id=1, source_target_pairs={{4,0},{8,4},{12,8},{16,12},{20,16},{24,20},{28,24},{5,1},{9,5},{13... | collective-permute-start | bytes 4718600 | tf_op jit(solution)/shard_map/ppermute | solution.py:14
  4.2 0.0 copy-done.2
  4.2 0.6 multiply_convert_fusion.1
  4.8 0.1 copy.13
  5.0 0.1 convert_element_type.35
  5.0 0.0 copy-done
  5.0 1.5 %fusion = bf16[128,3072]{1,0:T(8,128)(2,1)} fusion(bf16[128,512]{1,0:T(8,128)(2,1)S(1)} %convert_element_type.35, bf16[512,3072]{1,0:T(8,128)(2,1)S(1)} %copy-done, pred[]{:T(512)S(6)} %lt.12), kind=kOutput, calls=%fused_computation.2 | convolution fusion | flops 403439616 | bytes 4063233 | tf_op jit(solution)/shard_map/dot_general | solution.py:39
  6.5 2.8 %stack.25 = bf16[1,64,2,3072]{3,2,1,0:T(2,128)(2,1)} reshape(bf16[128,3072]{1,0:T(8,128)(2,1)} %fusion) | data formatting | bytes 1572864 | tf_op jit(solution)/shard_map/stack | solution.py:41
  9.4 0.0 collective-permute-done
  9.4 2.9 %fusion.1 = bf16[128,3072]{1,0:T(8,128)(2,1)} fusion(bf16[128,512]{1,0:T(8,128)(2,1)S(1)} %convert_element_type.35, bf16[256,3072]{1,0:T(8,128)(2,1)} %collective-permute-done, bf16[512,3072]{1,0:T(8,128)(2,1)S(1)} %copy-done, pred[]{:T(512)S(6)} %lt.14), kind=kOutput, calls=%fused_computation.3 | convolution fusion | flops 409731072 | bytes 5636097 | tf_op jit(solution)/shard_map/dot_general | solution.py:39
  12.3 0.0 copy-start.1
  12.3 2.2 %stack.26 = bf16[1,64,2,3072]{3,2,1,0:T(2,128)(2,1)S(1)} reshape(bf16[128,3072]{1,0:T(8,128)(2,1)} %fusion.1) | data formatting | bytes 1572864 | tf_op jit(solution)/shard_map/stack | solution.py:41
  14.5 0.0 copy-done.1
  14.5 2.1 %pad_maximum_fusion.2 = bf16[2,64,2,3072]{3,2,0,1:T(2,128)(2,1)S(1)} fusion(bf16[1,64,2,3072]{3,2,0,1:T(2,128)(2,1)S(1)} %bitcast.22, bf16[1,64,2,3072]{3,2,0,1:T(2,128)(2,1)S(1)} %bitcast.21), kind=kLoop, calls=%fused_computation.6 | loop fusion | flops 786432 | bytes 3145728 | tf_op jit(solution)/shard_map/stack | solution.py:41
  16.6 58.0 %all_to_all.18 = bf16[2,64,2,3072]{3,2,0,1:T(2,128)(2,1)S(1)} all-to-all(bf16[2,64,2,3072]{3,2,0,1:T(2,128)(2,1)S(1)} %pad_maximum_fusion.2), channel_id=1, replica_groups=mesh['tm'=8,'space'=4] {'tm'}, dimensions={1} | all-to-all | bytes 3145728 | tf_op jit(solution)/shard_map/all_to_all | solution.py:43
  74.6 1.7 %copy.16 = bf16[8,2,8,2,3072]{4,1,0,3,2:T(2,128)(2,1)S(1)} copy(bf16[8,2,8,2,3072]{4,3,1,2,0:T(2,128)(2,1)S(1)} %bitcast.20) | data formatting | bytes 3145728 | tf_op jit(solution)/shard_map/all_to_all | solution.py:43
  76.3 0.6 all_to_all.16
  76.9 0.5 fusion.14
  77.5 0.1 fusion.11
  77.6 18.4 %psum.7 = f32[8,2,15,15]{3,2,0,1:T(8,128)S(1)} all-reduce(f32[8,2,15,15]{3,2,0,1:T(8,128)S(1)} %fusion.6), channel_id=1, replica_groups=mesh['tm'=8,'space'=4] {'space'}, use_global_device_ids=true, to_apply=%region_0.1 | all-reduce | flops 3600 | bytes 28800 | tf_op jit(solution)/shard_map/psum | solution.py:67
  96.0 0.7 copy.17
  (3 shorter events, 0.1 us)
Async XLA Ops:
  0.0 5.0 %copy-start = (bf16[512,3072]{1,0:T(8,128)(2,1)S(1)}, bf16[512,3072]{1,0:T(8,128)(2,1)}, u32[]{:S(2)}) copy-start(bf16[512,3072]{1,0:T(8,128)(2,1)} %param.2) | copy-start | bytes 9437188
  0.0 4.2 %copy-start.2 = (s32[64]{0:T(128)S(1)}, s32[64]{0:T(128)}, u32[]{:S(2)}) copy-start(s32[64]{0:T(128)} %param.3) | copy-start | bytes 772
  2.8 6.5 %collective-permute-start = (bf16[256,3072]{1,0:T(8,128)(2,1)}, bf16[256,3072]{1,0:T(8,128)(2,1)}, u32[]{:S(2)}, u32[]{:S(2)}) collective-permute-start(bf16[256,3072]{1,0:T(8,128)(2,1)} %slice.21), channel_id=1, source_target_pairs={{4,0},{8,4},{12,8},{16,12},{20,16},{24,20},{28,24},{5,1},{9,5},{13... | collective-permute-start | bytes 4718600 | tf_op jit(solution)/shard_map/ppermute | solution.py:14
  12.3 2.2 %copy-start.1 = (bf16[1,64,2,3072]{3,2,1,0:T(2,128)(2,1)S(1)}, bf16[1,64,2,3072]{3,2,1,0:T(2,128)(2,1)}, u32[]{:S(2)}) copy-start(bf16[1,64,2,3072]{3,2,1,0:T(2,128)(2,1)} %stack.25) | copy-start | bytes 2359300
where the time goes:
time: 97 us; the launch traced here: 96.8 us
  blocking collectives  76.4 us (79%)
  local copies, waits for them, and re-layouts  11.2 us (12%)
  matrix products  4.92 us (5%)
  other arithmetic  2.86 us (3%)
  starting transfers between devices  1.28 us (1%)
    all_to_all x1, blocking collectives, local(): lax.all_to_all(owned, 'tm', split_axis=1, concat_axis=0, tiled=True)  58 us
    psum x1, blocking collectives, local(): return lax.psum(resident_gram_matrix, 'space')  18.4 us
    another operation x2, local copies, waits for them, and re-layouts, local(): owned = jnp.stack(pieces, axis=0).astype(jnp.bfloat16)  5.07 us
    dot_general x2, matrix products, local(): result = jnp.dot(table, segment, preferred_element_type=jnp.float32)  4.38 us
    slice x1, local copies, waits for them, and re-layouts, local(): leading = shifted(snapshots[:hop_len], 'tm', -1)  2.83 us
    all_to_all x2, local copies, waits for them, and re-layouts, local(): lax.all_to_all(owned, 'tm', split_axis=1, concat_axis=0, tiled=True)  2.33 us
    another operation x1, other arithmetic, local(): owned = jnp.stack(pieces, axis=0).astype(jnp.bfloat16)  2.07 us
  transfers between devices with their start and end apart: 1, of which 0 were waited for; matrix products, arithmetic and copies ran while one was open for 5% of the time, Pallas kernels for 0%

commit v1 on v0

--- a/solution.py
+++ b/solution.py
@@ -6,6 +6,18 @@
 
 NFFT = 512
 F = 64
+
+
+def cut_along(shard, dim, devices):
+    shape = shard.shape
+    parts = shard.reshape(*shape[:dim], devices, shape[dim] // devices, *shape[dim + 1 :])
+    return jnp.moveaxis(parts, dim, 0)
+
+
+def in_order(pieces, dim):
+    pieces = jnp.moveaxis(pieces, 0, dim)
+    dims = pieces.shape
+    return pieces.reshape(*dims[:dim], dims[dim] * dims[dim + 1], *dims[dim + 2 :])
 
 
 def shifted(block, axis, distance):
@@ -40,7 +52,15 @@
         pieces.append(jnp.where(block < blocks, result, 0.0))
     owned = jnp.stack(pieces, axis=0).astype(jnp.bfloat16)
     owned = owned.reshape(2, F, 2, points)
-    by_freq = lax.all_to_all(owned, "tm", split_axis=1, concat_axis=0, tiled=True)
+    size, mine = (lax.axis_size("tm"), lax.axis_index("tm"))
+    tiles = cut_along(owned, 1, size)
+    out = tiles
+    for step in range(1, size):
+        target, source = ((mine + step) % size, (mine - step) % size)
+        sent = lax.dynamic_index_in_dim(tiles, target, 0)
+        received = lax.ppermute(sent, "tm", [(i_2, (i_2 + step) % size) for i_2 in range(size)])
+        out = lax.dynamic_update_slice_in_dim(out, received, source, axis=0)
+    by_freq = in_order(out, 0)
     slots_all = by_freq.shape[0]
     resident_frequencies = by_freq.shape[1]
     stacked_snapshot_rows = jnp.transpose(by_freq, (1, 2, 0, 3)).reshape(

time: 97 us -> 85.5 us (0.88)
  the two profiles are of different devices: /device:TPU:0 before, /device:TPU:8 now
where the time goes in v1:
time: 85.5 us; the launch traced here: 85.3 us
  waiting for transfers between devices  43.6 us (51%)
  blocking collectives  18.8 us (22%)
  starting transfers between devices  9.71 us (11%)
  local copies, waits for them, and re-layouts  7.63 us (9%)
  matrix products  4.48 us (5%)
    ppermute x7, waiting for transfers between devices, local(): lax.ppermute(sent, 'tm', [(i_2, (i_2 + step) % size) for i_2 in range(siz...  28.1 us
    psum x1, blocking collectives, local(): return lax.psum(resident_gram_matrix, 'space')  18.8 us
    ppermute x1, waiting for transfers between devices, shifted(): return lax.ppermute(block, axis, route)  15.5 us
    ppermute x7, starting transfers between devices, local(): lax.ppermute(sent, 'tm', [(i_2, (i_2 + step) % size) for i_2 in range(siz...  7.8 us
    dot_general x2, matrix products, local(): result = jnp.dot(table, segment, preferred_element_type=jnp.float32)  3.95 us
    slice x1, local copies, waits for them, and re-layouts, local(): leading = shifted(snapshots[:hop_len], 'tm', -1)  2.83 us
    another operation x3, local copies, waits for them, and re-layouts, local(): owned = jnp.stack(pieces, axis=0).astype(jnp.bfloat16)  2.6 us
    ppermute x1, starting transfers between devices, shifted(): return lax.ppermute(block, axis, route)  1.91 us
  transfers between devices with their start and end apart: 8, of which 5 were waited for; matrix products, arithmetic and copies ran while one was open for 6% of the time, Pallas kernels for 0%

profile of v1, /device:TPU:8, one launch (start us, length us, event | category | flops | bytes accessed | tf_op | source)
XLA Modules:
  0.0 85.3 jit_solution(16886957333334401100)
XLA Ops:
  0.0 2.8 %slice.21 = bf16[256,3072]{1,0:T(8,128)(2,1)} slice(bf16[512,3072]{1,0:T(8,128)(2,1)} %param.2), slice={[0:256], [0:3072]} | slice | bytes 3145728 | tf_op jit(solution)/shard_map/slice | solution.py:45
  2.8 1.9 %collective-permute-start = (bf16[256,3072]{1,0:T(8,128)(2,1)}, bf16[256,3072]{1,0:T(8,128)(2,1)}, u32[]{:S(2)}, u32[]{:S(2)}) collective-permute-start(bf16[256,3072]{1,0:T(8,128)(2,1)} %slice.21), channel_id=1, source_target_pairs={{4,0},{8,4},{12,8},{16,12},{20,16},{24,20},{28,24},{5,1},{9,5},{13... | collective-permute-start | bytes 4718600 | tf_op jit(solution)/shard_map/ppermute | solution.py:26
  4.9 0.6 multiply_convert_fusion.1
  5.5 0.1 copy.15
  5.7 0.1 convert_element_type.35
  5.7 1.5 %fusion = bf16[128,3072]{1,0:T(8,128)(2,1)} fusion(bf16[128,512]{1,0:T(8,128)(2,1)S(1)} %convert_element_type.35, bf16[512,3072]{1,0:T(8,128)(2,1)S(1)} %copy-done, pred[]{:T(512)S(6)} %lt.113), kind=kOutput, calls=%fused_computation.2 | convolution fusion | flops 403439616 | bytes 4063233 | tf_op jit(solution)/shard_map/dot_general | solution.py:51
  7.2 2.2 %stack.25 = bf16[1,8,8,2,3072]{4,3,2,1,0:T(2,128)(2,1)S(1)} reshape(bf16[128,3072]{1,0:T(8,128)(2,1)} %fusion) | data formatting | bytes 1572864 | tf_op jit(solution)/shard_map/stack | solution.py:53
  9.4 0.1 copy_dynamic-update-slice_fusion.1
  9.6 15.5 %collective-permute-done = bf16[256,3072]{1,0:T(8,128)(2,1)} collective-permute-done((bf16[256,3072]{1,0:T(8,128)(2,1)}, bf16[256,3072]{1,0:T(8,128)(2,1)}, u32[]{:S(2)}, u32[]{:S(2)}) %collective-permute-start) | collective-permute-done | bytes 1572896 | tf_op jit(solution)/shard_map/ppermute | solution.py:26
  25.1 2.5 %fusion.1 = bf16[128,3072]{1,0:T(8,128)(2,1)S(1)} fusion(bf16[128,512]{1,0:T(8,128)(2,1)S(1)} %convert_element_type.35, bf16[256,3072]{1,0:T(8,128)(2,1)} %collective-permute-done, bf16[512,3072]{1,0:T(8,128)(2,1)} %param.2, pred[]{:T(512)S(6)} %lt.115), kind=kOutput, calls=%fused_computation.3 | convolution fusion | flops 409731072 | bytes 5636097 | tf_op jit(solution)/shard_map/dot_general | solution.py:51
  27.6 0.3 stack.26
  27.9 0.1 copy_dynamic-update-slice_fusion
  28.0 0.1 dynamic-slice_bitcast_fusion
  28.1 1.9 %collective-permute-start.1 = (bf16[1,2,8,2,3072]{4,2,3,1,0:T(8,128)(2,1)S(1)}, bf16[1,2,8,2,3072]{4,2,3,1,0:T(8,128)(2,1)S(1)}, u32[]{:S(2)}, u32[]{:S(2)}) collective-permute-start(bf16[1,2,8,2,3072]{4,2,3,1,0:T(8,128)(2,1)S(1)} %get-tuple-element.11), channel_id=1, source_target_pairs={{0,4},{4,8},{8,12},{12,16},{16,20},{20,24},{24,28},{28,0},{1,5},{5... | collective-permute-start | bytes 589832 | tf_op jit(solution)/shard_map/ppermute | solution.py:61
  30.0 1.6 %collective-permute-start.2 = (bf16[1,2,8,2,3072]{4,2,3,1,0:T(8,128)(2,1)S(1)}, bf16[1,2,8,2,3072]{4,2,3,1,0:T(8,128)(2,1)S(1)}, u32[]{:S(2)}, u32[]{:S(2)}) collective-permute-start(bf16[1,2,8,2,3072]{4,2,3,1,0:T(8,128)(2,1)S(1)} %get-tuple-element.10), channel_id=1, source_target_pairs={{0,8},{4,12},{8,16},{12,20},{16,24},{20,28},{24,0},{28,4},{1,9},{5... | collective-permute-start | bytes 589832 | tf_op jit(solution)/shard_map/ppermute | solution.py:61
  31.6 0.0 collective-permute-start.3
  31.6 2.3 %collective-permute-start.4 = (bf16[1,2,8,2,3072]{4,2,3,1,0:T(8,128)(2,1)S(1)}, bf16[1,2,8,2,3072]{4,2,3,1,0:T(8,128)(2,1)S(1)}, u32[]{:S(2)}, u32[]{:S(2)}) collective-permute-start(bf16[1,2,8,2,3072]{4,2,3,1,0:T(8,128)(2,1)S(1)} %get-tuple-element.8), channel_id=1, source_target_pairs={{0,16},{4,20},{8,24},{12,28},{16,0},{20,4},{24,8},{28,12},{1,17},{... | collective-permute-start | bytes 589832 | tf_op jit(solution)/shard_map/ppermute | solution.py:61
  34.0 1.3 %collective-permute-start.5 = (bf16[1,2,8,2,3072]{4,2,3,1,0:T(8,128)(2,1)S(1)}, bf16[1,2,8,2,3072]{4,2,3,1,0:T(8,128)(2,1)S(1)}, u32[]{:S(2)}, u32[]{:S(2)}) collective-permute-start(bf16[1,2,8,2,3072]{4,2,3,1,0:T(8,128)(2,1)S(1)} %get-tuple-element.7), channel_id=1, source_target_pairs={{0,20},{4,24},{8,28},{12,0},{16,4},{20,8},{24,12},{28,16},{1,21},{... | collective-permute-start | bytes 589832 | tf_op jit(solution)/shard_map/ppermute | solution.py:61
  35.2 0.0 collective-permute-done.1
  35.2 0.2 collective-permute-start.6
  35.5 2.3 %collective-permute-done.2 = bf16[1,2,8,2,3072]{4,2,3,1,0:T(8,128)(2,1)S(1)} collective-permute-done((bf16[1,2,8,2,3072]{4,2,3,1,0:T(8,128)(2,1)S(1)}, bf16[1,2,8,2,3072]{4,2,3,1,0:T(8,128)(2,1)S(1)}, u32[]{:S(2)}, u32[]{:S(2)}) %collective-permute-start.2) | collective-permute-done | bytes 196640 | tf_op jit(solution)/shard_map/ppermute | solution.py:61
  37.8 0.5 collective-permute-start.7
  38.3 19.6 %collective-permute-done.3 = bf16[1,2,8,2,3072]{4,2,3,1,0:T(8,128)(2,1)S(1)} collective-permute-done((bf16[1,2,8,2,3072]{4,2,3,1,0:T(8,128)(2,1)S(1)}, bf16[1,2,8,2,3072]{4,2,3,1,0:T(8,128)(2,1)S(1)}, u32[]{:S(2)}, u32[]{:S(2)}) %collective-permute-start.3) | collective-permute-done | bytes 196640 | tf_op jit(solution)/shard_map/ppermute | solution.py:61
  58.0 4.0 %collective-permute-done.4 = bf16[1,2,8,2,3072]{4,2,3,1,0:T(8,128)(2,1)S(1)} collective-permute-done((bf16[1,2,8,2,3072]{4,2,3,1,0:T(8,128)(2,1)S(1)}, bf16[1,2,8,2,3072]{4,2,3,1,0:T(8,128)(2,1)S(1)}, u32[]{:S(2)}, u32[]{:S(2)}) %collective-permute-start.4) | collective-permute-done | bytes 196640 | tf_op jit(solution)/shard_map/ppermute | solution.py:61
  62.1 2.1 %collective-permute-done.5 = bf16[1,2,8,2,3072]{4,2,3,1,0:T(8,128)(2,1)S(1)} collective-permute-done((bf16[1,2,8,2,3072]{4,2,3,1,0:T(8,128)(2,1)S(1)}, bf16[1,2,8,2,3072]{4,2,3,1,0:T(8,128)(2,1)S(1)}, u32[]{:S(2)}, u32[]{:S(2)}) %collective-permute-start.5) | collective-permute-done | bytes 196640 | tf_op jit(solution)/shard_map/ppermute | solution.py:61
  64.2 0.0 collective-permute-done.6
  64.2 0.0 collective-permute-done.7
  64.2 0.9 %copy.18 = bf16[8,2,16,3072]{3,2,1,0:T(8,128)(2,1)S(1)} copy(bf16[8,2,16,3072]{3,0,1,2:T(8,128)(2,1)S(1)} %bitcast.30) | data formatting | bytes 3145728 | tf_op jit(solution)/shard_map/transpose | solution.py:66
  65.1 0.5 fusion.14
  65.7 0.1 fusion.11
  65.8 18.8 %psum.7 = f32[8,2,15,15]{3,2,0,1:T(8,128)S(1)} all-reduce(f32[8,2,15,15]{3,2,0,1:T(8,128)S(1)} %fusion.6), channel_id=1, replica_groups=mesh['tm'=8,'space'=4] {'space'}, use_global_device_ids=true, to_apply=%region_0.1 | all-reduce | flops 3600 | bytes 28800 | tf_op jit(solution)/shard_map/psum | solution.py:87
  84.6 0.7 copy.19
  (14 shorter events, 0.2 us)
Async XLA Ops:
  0.0 5.7 %copy-start = (bf16[512,3072]{1,0:T(8,128)(2,1)S(1)}, bf16[512,3072]{1,0:T(8,128)(2,1)}, u32[]{:S(2)}) copy-start(bf16[512,3072]{1,0:T(8,128)(2,1)} %param.2) | copy-start | bytes 9437188
  0.0 4.9 %copy-start.1 = (s32[64]{0:T(128)S(1)}, s32[64]{0:T(128)}, u32[]{:S(2)}) copy-start(s32[64]{0:T(128)} %param.3) | copy-start | bytes 772
  2.8 22.3 %collective-permute-start = (bf16[256,3072]{1,0:T(8,128)(2,1)}, bf16[256,3072]{1,0:T(8,128)(2,1)}, u32[]{:S(2)}, u32[]{:S(2)}) collective-permute-start(bf16[256,3072]{1,0:T(8,128)(2,1)} %slice.21), channel_id=1, source_target_pairs={{4,0},{8,4},{12,8},{16,12},{20,16},{24,20},{28,24},{5,1},{9,5},{13... | collective-permute-start | bytes 4718600 | tf_op jit(solution)/shard_map/ppermute | solution.py:26
  28.1 7.1 %collective-permute-start.1 = (bf16[1,2,8,2,3072]{4,2,3,1,0:T(8,128)(2,1)S(1)}, bf16[1,2,8,2,3072]{4,2,3,1,0:T(8,128)(2,1)S(1)}, u32[]{:S(2)}, u32[]{:S(2)}) collective-permute-start(bf16[1,2,8,2,3072]{4,2,3,1,0:T(8,128)(2,1)S(1)} %get-tuple-element.11), channel_id=1, source_target_pairs={{0,4},{4,8},{8,12},{12,16},{16,20},{20,24},{24,28},{28,0},{1,5},{5... | collective-permute-start | bytes 589832 | tf_op jit(solution)/shard_map/ppermute | solution.py:61
  30.0 7.8 %collective-permute-start.2 = (bf16[1,2,8,2,3072]{4,2,3,1,0:T(8,128)(2,1)S(1)}, bf16[1,2,8,2,3072]{4,2,3,1,0:T(8,128)(2,1)S(1)}, u32[]{:S(2)}, u32[]{:S(2)}) collective-permute-start(bf16[1,2,8,2,3072]{4,2,3,1,0:T(8,128)(2,1)S(1)} %get-tuple-element.10), channel_id=1, source_target_pairs={{0,8},{4,12},{8,16},{12,20},{16,24},{20,28},{24,0},{28,4},{1,9},{5... | collective-permute-start | bytes 589832 | tf_op jit(solution)/shard_map/ppermute | solution.py:61
  31.6 26.4 %collective-permute-start.3 = (bf16[1,2,8,2,3072]{4,2,3,1,0:T(8,128)(2,1)S(1)}, bf16[1,2,8,2,3072]{4,2,3,1,0:T(8,128)(2,1)S(1)}, u32[]{:S(2)}, u32[]{:S(2)}) collective-permute-start(bf16[1,2,8,2,3072]{4,2,3,1,0:T(8,128)(2,1)S(1)} %get-tuple-element.9), channel_id=1, source_target_pairs={{0,12},{4,16},{8,20},{12,24},{16,28},{20,0},{24,4},{28,8},{1,13},{... | collective-permute-start | bytes 589832 | tf_op jit(solution)/shard_map/ppermute | solution.py:61
  31.6 30.4 %collective-permute-start.4 = (bf16[1,2,8,2,3072]{4,2,3,1,0:T(8,128)(2,1)S(1)}, bf16[1,2,8,2,3072]{4,2,3,1,0:T(8,128)(2,1)S(1)}, u32[]{:S(2)}, u32[]{:S(2)}) collective-permute-start(bf16[1,2,8,2,3072]{4,2,3,1,0:T(8,128)(2,1)S(1)} %get-tuple-element.8), channel_id=1, source_target_pairs={{0,16},{4,20},{8,24},{12,28},{16,0},{20,4},{24,8},{28,12},{1,17},{... | collective-permute-start | bytes 589832 | tf_op jit(solution)/shard_map/ppermute | solution.py:61
  34.0 30.2 %collective-permute-start.5 = (bf16[1,2,8,2,3072]{4,2,3,1,0:T(8,128)(2,1)S(1)}, bf16[1,2,8,2,3072]{4,2,3,1,0:T(8,128)(2,1)S(1)}, u32[]{:S(2)}, u32[]{:S(2)}) collective-permute-start(bf16[1,2,8,2,3072]{4,2,3,1,0:T(8,128)(2,1)S(1)} %get-tuple-element.7), channel_id=1, source_target_pairs={{0,20},{4,24},{8,28},{12,0},{16,4},{20,8},{24,12},{28,16},{1,21},{... | collective-permute-start | bytes 589832 | tf_op jit(solution)/shard_map/ppermute | solution.py:61
  35.2 28.9 %collective-permute-start.6 = (bf16[1,2,8,2,3072]{4,2,3,1,0:T(8,128)(2,1)S(1)}, bf16[1,2,8,2,3072]{4,2,3,1,0:T(8,128)(2,1)S(1)}, u32[]{:S(2)}, u32[]{:S(2)}) collective-permute-start(bf16[1,2,8,2,3072]{4,2,3,1,0:T(8,128)(2,1)S(1)} %get-tuple-element.6), channel_id=1, source_target_pairs={{0,24},{4,28},{8,0},{12,4},{16,8},{20,12},{24,16},{28,20},{1,25},{... | collective-permute-start | bytes 589832 | tf_op jit(solution)/shard_map/ppermute | solution.py:61
  37.8 26.4 %collective-permute-start.7 = (bf16[1,2,8,2,3072]{4,2,3,1,0:T(8,128)(2,1)S(1)}, bf16[1,2,8,2,3072]{4,2,3,1,0:T(8,128)(2,1)S(1)}, u32[]{:S(2)}, u32[]{:S(2)}) collective-permute-start(bf16[1,2,8,2,3072]{4,2,3,1,0:T(8,128)(2,1)S(1)} %get-tuple-element.5), channel_id=1, source_target_pairs={{0,28},{4,0},{8,4},{12,8},{16,12},{20,16},{24,20},{28,24},{1,29},{... | collective-permute-start | bytes 589832 | tf_op jit(solution)/shard_map/ppermute | solution.py:61
